TPU v7x, 32 devices: a whole 2x2x4 slice. The times are simulated.
32 devices in a mesh: dp: 8 (over z, y), ctx: 4 (over x, core).
Axes of the slice: x: 2, y: 2, z: 4, core: 2. Of those that a mesh axis runs over, the one named last changes fastest.
Arguments:
- projected: bfloat16 [8, 512, 3, 4096], P('dp', 'ctx'), may hold values from -6 to 6
- short_taps: float32 [3, 3, 4096], P(None, None, 'ctx'), may hold values from -3 to 3
- long_filter: bfloat16 [512, 4096], P('dp', 'ctx'), may hold values from -1.1 to 1.1
- skip_gain: float32 [4096], P('ctx'), may hold values from -4 to 4
Outputs:
- mixed: bfloat16 [8, 512, 4096], P('dp', 'ctx')
All inputs are finite; a program needn't handle non-finite values.
Results may differ from a plain program's by a relative error of at most 0.012.
Values may be sent and summed in bfloat16 or wider, within the bound.
A program may use at most 64 MiB of HBM per device.

v0:
```python
import math
import jax
import jax.numpy as jnp
import numpy as np
from jax import lax
from jax.sharding import PartitionSpec as P

RADIX = 64
HIGH = lax.Precision.HIGHEST


def causal_short(extended, taps, kernel_size):
    row_count = extended.shape[0] - (kernel_size - 1)
    widened = extended.astype(jnp.float32)
    summed = jnp.zeros((row_count,) + widened.shape[1:], jnp.float32)
    for tap_index in range(kernel_size):
        offset = kernel_size - 1 - tap_index
        summed = summed + taps[tap_index] * widened[offset : offset + row_count]
    return (summed[:, 0].astype(jnp.bfloat16), (summed[:, 1] * summed[:, 2]).astype(jnp.bfloat16))


def dft_tables(length, radix_size):
    outer_size = 2 * length // radix_size
    total_size = outer_size * radix_size
    outer_range = jnp.arange(outer_size, dtype=jnp.int32)
    inner_range = jnp.arange(radix_size, dtype=jnp.int32)
    angle_one = (
        2.0
        * math.pi
        / outer_size
        * (outer_range[:, None] * outer_range[None, :] % outer_size).astype(jnp.float32)
    )
    angle_twist = (
        2.0
        * math.pi
        / total_size
        * (outer_range[:, None] * inner_range[None, :] % total_size).astype(jnp.float32)
    )
    angle_two = (
        2.0
        * math.pi
        / radix_size
        * (inner_range[:, None] * inner_range[None, :] % radix_size).astype(jnp.float32)
    )
    twist_cos = jnp.cos(angle_twist)[:, :, None]
    twist_sin = jnp.sin(angle_twist)[:, :, None]
    return (
        jnp.cos(angle_one),
        jnp.sin(angle_one),
        twist_cos,
        twist_sin,
        jnp.cos(angle_two),
        jnp.sin(angle_two),
    )


def forward_dft(signal, tables, radix_size):
    cos_one, sin_one, twist_cos, twist_sin, cos_two, sin_two = tables
    outer_size = cos_one.shape[0]
    half_size = outer_size // 2
    block_width = signal.shape[1]
    shaped = signal.reshape(half_size, radix_size * block_width)
    first_re = jnp.dot(cos_one[:, :half_size], shaped, precision=HIGH).reshape(
        outer_size, radix_size, block_width
    )
    first_im = -jnp.dot(sin_one[:, :half_size], shaped, precision=HIGH).reshape(
        outer_size, radix_size, block_width
    )
    second_re = first_re * twist_cos + first_im * twist_sin
    second_im = first_im * twist_cos - first_re * twist_sin
    spec_re = jnp.einsum("amc,mb->abc", second_re, cos_two, precision=HIGH) + jnp.einsum(
        "amc,mb->abc", second_im, sin_two, precision=HIGH
    )
    spec_im = jnp.einsum("amc,mb->abc", second_im, cos_two, precision=HIGH) - jnp.einsum(
        "amc,mb->abc", second_re, sin_two, precision=HIGH
    )
    return (spec_re, spec_im)


def inverse_dft(spec_re, spec_im, tables, radix_size):
    cos_one, sin_one, twist_cos, twist_sin, cos_two, sin_two = tables
    outer_size = cos_one.shape[0]
    half_size = outer_size // 2
    block_width = spec_re.shape[2]
    back_re = jnp.einsum("abc,mb->amc", spec_re, cos_two, precision=HIGH) - jnp.einsum(
        "abc,mb->amc", spec_im, sin_two, precision=HIGH
    )
    back_im = jnp.einsum("abc,mb->amc", spec_re, sin_two, precision=HIGH) + jnp.einsum(
        "abc,mb->amc", spec_im, cos_two, precision=HIGH
    )
    turned_re = (back_re * twist_cos - back_im * twist_sin).reshape(
        outer_size, radix_size * block_width
    )
    turned_im = (back_re * twist_sin + back_im * twist_cos).reshape(
        outer_size, radix_size * block_width
    )
    result = jnp.dot(cos_one[:half_size], turned_re, precision=HIGH) - jnp.dot(
        sin_one[:half_size], turned_im, precision=HIGH
    )
    return result.reshape(half_size * radix_size, block_width) / (outer_size * radix_size)


def long_convolve_blocked(gated_slab, filter_slab):
    length, channels = gated_slab.shape
    block_width = min(128, channels)
    tables = dft_tables(length, RADIX)

    def one_block(block_index, output):
        offset = block_index * block_width
        signal = lax.dynamic_slice_in_dim(gated_slab, offset, block_width, 1).astype(jnp.float32)
        kernel_block = lax.dynamic_slice_in_dim(filter_slab, offset, block_width, 1).astype(
            jnp.float32
        )
        sig_re, sig_im = forward_dft(signal, tables, RADIX)
        ker_re, ker_im = forward_dft(kernel_block, tables, RADIX)
        prod_re = sig_re * ker_re - sig_im * ker_im
        prod_im = sig_re * ker_im + sig_im * ker_re
        result = inverse_dft(prod_re, prod_im, tables, RADIX)
        return lax.dynamic_update_slice_in_dim(output, result, offset, 1)

    return lax.fori_loop(
        0, channels // block_width, one_block, jnp.zeros((length, channels), jnp.float32)
    )


def long_convolve(gated_slab, filter_slab):
    length = gated_slab.shape[0]
    if length > 1024:
        return long_convolve_blocked(gated_slab, filter_slab)
    forward, backward = quarter_tables(length)
    sig = jnp.dot(forward, gated_slab, preferred_element_type=jnp.float32)
    ker = jnp.dot(forward, filter_slab, preferred_element_type=jnp.float32)
    sig_cos, sig_sin, ker_cos, ker_sin = (sig[:length], sig[length:], ker[:length], ker[length:])
    prod = jnp.concatenate(
        [sig_cos * ker_cos - sig_sin * ker_sin, sig_cos * ker_sin + sig_sin * ker_cos]
    ).astype(jnp.bfloat16)
    return jnp.dot(backward, prod, preferred_element_type=jnp.float32)


def quarter_tables(length):
    steps = (4 * np.arange(length)[:, None] + 1) * np.arange(length)[None, :] % (4 * length)
    angles = steps * (2.0 * math.pi / (4 * length))
    table = np.concatenate([np.cos(angles), np.sin(angles)])
    return (jnp.asarray(table, jnp.bfloat16), jnp.asarray(table.T / length, jnp.bfloat16))


def make_response(gated_slab, filter_slab, skip_gain):
    long_part = long_convolve(gated_slab, filter_slab)
    return (long_part + skip_gain * gated_slab.astype(jnp.float32)).astype(jnp.bfloat16)


def combine_rows(query_part, response_part):
    return (query_part.astype(jnp.float32) * response_part.astype(jnp.float32)).astype(jnp.bfloat16)


def on_device(projected, short_taps, long_filter, skip_gain):
    kernel_size = short_taps.shape[0]
    ctx_size = lax.axis_size("ctx")
    rows = projected[0]
    filter_slab = lax.all_gather(long_filter, "dp", axis=0, tiled=True)
    all_taps = lax.all_gather(short_taps, "ctx", axis=2, tiled=True)
    halo = lax.ppermute(
        rows[-(kernel_size - 1) :], "ctx", [(i, i + 1) for i in range(ctx_size - 1)]
    )
    queries, gated = causal_short(jnp.concatenate([halo, rows]), all_taps, kernel_size)
    gated_slab = lax.all_to_all(gated, "ctx", split_axis=1, concat_axis=0, tiled=True)
    response_slab = make_response(gated_slab, filter_slab, skip_gain)
    response = lax.all_to_all(response_slab, "ctx", split_axis=0, concat_axis=1, tiled=True)
    return combine_rows(queries, response)[None]


def solution(mesh):
    return jax.shard_map(
        on_device,
        mesh=mesh,
        in_specs=(P("dp", "ctx", None, None), P(None, None, "ctx"), P("dp", "ctx"), P("ctx")),
        out_specs=P("dp", "ctx", None),
        check_vma=False,
    )
```

profile of v0, /device:TPU:0, one launch (start us, length us, event | category | flops | bytes accessed | tf_op | source)
XLA Modules:
  0.0 98.3 jit_solution(9374394444664084530)
XLA Ops:
  6.5 0.0 all-gather.2.cloned.1.call-start
  6.5 1.0 slice_bitcast_fusion.3
  7.5 2.4 %collective-permute-start = (bf16[2,3,4096]{2,0,1:T(2,128)(2,1)S(1)}, bf16[2,3,4096]{2,0,1:T(2,128)(2,1)S(1)}, u32[]{:S(2)}, u32[]{:S(2)}) collective-permute-start(bf16[2,3,4096]{2,0,1:T(2,128)(2,1)S(1)} %slice_bitcast_fusion.3), channel_id=1, source_target_pairs={{0,1},{1,2},{2,3},{4,5},{5,6},{6,7},{8,9},{9,10},{10,11},{12,13},{... | collective-permute-start | bytes 147464 | tf_op jit(solution)/shard_map/ppermute | solution.py:162
  9.9 0.0 all-gather.2.cloned.1.call-update
  9.9 7.1 %all_gather.6 = f32[3,3,4096]{2,1,0:T(4,128)S(1)} all-gather(f32[3,3,1024]{2,1,0:T(4,128)} %param.7), channel_id=1, replica_groups=mesh['dp'=8,'ctx'=4] {'ctx'}, dimensions={2}, use_global_device_ids=true | all-gather | bytes 184320 | tf_op jit(solution)/shard_map/all_gather | solution.py:161
  17.1 3.5 %copy.19 = bf16[1,128,3,4096]{1,3,2,0:T(8,128)(2,1)S(1)} copy(bf16[1,128,3,4096]{3,1,2,0:T(8,128)(2,1)} %param.6) | data formatting | bytes 6291456 | tf_op args[0]
  20.6 0.0 collective-permute-done
  20.6 2.8 %copy.20 = bf16[2,3,4096]{0,2,1:T(8,128)(2,1)} copy(bf16[2,3,4096]{2,0,1:T(2,128)(2,1)S(1)} %collective-permute-done) | data formatting | bytes 98304 | tf_op jit(solution)/shard_map/ppermute | solution.py:162
  23.4 4.1 %maximum_convert_fusion = f32[130,3,4096]{0,2,1:T(8,128)S(1)} fusion(bf16[128,3,4096]{0,2,1:T(8,128)(2,1)S(1)} %bitcast.36, bf16[2,3,4096]{0,2,1:T(8,128)(2,1)} %copy.20), kind=kLoop, calls=%fused_computation.5 | loop fusion | flops 6389760 | bytes 9584640 | tf_op jit(solution)/shard_map/convert_element_type | solution.py:14
  27.5 9.4 %fusion = f32[128,3,4096]{0,2,1:T(8,128)S(1)} fusion(f32[130,3,4096]{0,2,1:T(8,128)S(1)} %maximum_convert_fusion, f32[3,4096]{1,0:T(4,128)S(1)} %get-tuple-element.6, f32[3,4096]{1,0:T(4,128)S(1)} %get-tuple-element.7, f32[3,4096]{1,0:T(4,128)S(1)} %get-tuple-element.5), kind=kLoop, calls=%fused_computation.1 | loop fusion | flops 7864320 | bytes 25313280 | tf_op jit(solution)/shard_map/add | solution.py:18
  36.9 0.0 copy-start
  36.9 2.7 %copy-done = f32[128,3,4096]{0,2,1:T(8,128)} copy-done((f32[128,3,4096]{0,2,1:T(8,128)}, f32[128,3,4096]{0,2,1:T(8,128)S(1)}, u32[]{:S(2)}) %copy-start) | copy-done | bytes 6291480
  39.5 0.2 fusion.2
  39.7 0.5 copy.21
  40.3 16.9 %all_to_all.29 = bf16[128,4,1024]{2,0,1:T(8,128)(2,1)S(1)} all-to-all(bf16[128,4,1024]{2,0,1:T(8,128)(2,1)S(1)} %copy.21), channel_id=1, replica_groups=mesh['dp'=8,'ctx'=4] {'ctx'}, dimensions={1} | all-to-all | bytes 2097152 | tf_op jit(solution)/shard_map/all_to_all | solution.py:166
  57.2 0.8 copy.22
  58.0 0.3 reshape.46
  58.3 4.5 %fusion.8 = f32[1024,1024]{1,0:T(8,128)} fusion(bf16[1024,512]{1,0:T(8,128)(2,1)} %constant.9, bf16[512,1024]{1,0:T(8,128)(2,1)S(1)} %reshape.46), kind=kOutput, calls=%fused_computation.23 | convolution fusion | flops 1073741824 | bytes 6291456 | tf_op jit(solution)/shard_map/dot_general | solution.py:131
  62.8 0.0 copy-start.3
  62.8 0.0 all-gather.2.cloned.1.call-done
  62.8 0.0 copy-start.1
  62.8 2.9 %fusion.9 = f32[1024,1024]{1,0:T(8,128)S(1)} fusion(bf16[1024,512]{1,0:T(8,128)(2,1)} %constant.4.clone, bf16[512,1024]{1,0:T(8,128)(2,1)} %all-gather.2.cloned.1.call-done), kind=kOutput, calls=%fused_computation.24 | convolution fusion | flops 1073741824 | bytes 6291456 | tf_op jit(solution)/shard_map/dot_general | solution.py:132
  65.7 0.0 copy-done.3
  65.7 0.0 copy-done.1
  65.8 0.0 copy-start.2
  65.8 0.0 copy-start.4
  65.8 0.8 fusion.6
  66.6 0.2 copy-done.2
  66.8 0.0 copy-done.4
  66.8 0.9 fusion.4
  67.7 16.9 %all_to_all.30 = bf16[4,128,1024]{2,1,0:T(8,128)(2,1)S(1)} all-to-all(bf16[4,128,1024]{2,1,0:T(8,128)(2,1)S(1)} %bitcast.38), channel_id=1, replica_groups=mesh['dp'=8,'ctx'=4] {'ctx'}, dimensions={0} | all-to-all | bytes 2097152 | tf_op jit(solution)/shard_map/all_to_all | solution.py:168
  84.6 1.6 %convert_bitcast_fusion = f32[128,4,1024]{2,0,1:T(8,128)} fusion(bf16[4,128,1024]{2,1,0:T(8,128)(2,1)S(1)} %all_to_all.30), kind=kLoop, calls=%fused_computation.14 | loop fusion | flops 524288 | bytes 3145728 | tf_op jit(solution)/shard_map/convert_element_type | solution.py:153
  86.1 1.9 %copy.23 = f32[128,4,1024]{0,2,1:T(8,128)S(1)} copy(f32[128,4,1024]{2,0,1:T(8,128)} %convert_bitcast_fusion) | data formatting | bytes 4194304 | tf_op jit(solution)/shard_map/convert_element_type | solution.py:153
  88.1 2.0 %fusion.5 = bf16[1,128,4096]{1,2,0:T(8,128)(2,1)S(1)} fusion(f32[128,4,1024]{0,2,1:T(8,128)S(1)} %copy.23, f32[128,3,4096]{0,2,1:T(8,128)} %copy-done), kind=kLoop, calls=%fused_computation.13 | loop fusion | flops 1572864 | bytes 4194304 | tf_op jit(solution)/shard_map/convert_element_type | solution.py:153
  90.1 1.3 %copy.24 = bf16[1,128,4096]{2,1,0:T(8,128)(2,1)} copy(bf16[1,128,4096]{1,2,0:T(8,128)(2,1)S(1)} %fusion.5) | data formatting | bytes 2097152 | tf_op jit(solution)/shard_map/convert_element_type | solution.py:153
  (1 shorter events, 0.0 us)
Async XLA Ops:
  6.5 56.2 %all-gather.2.cloned.1.call-start = ((), (), s32[]{:S(2)}) async-start(), calls=%async_computation.2 | async-start | bytes 1179648 | tf_op jit(solution)/shard_map/all_gather | solution.py:160
  7.5 13.0 %collective-permute-start = (bf16[2,3,4096]{2,0,1:T(2,128)(2,1)S(1)}, bf16[2,3,4096]{2,0,1:T(2,128)(2,1)S(1)}, u32[]{:S(2)}, u32[]{:S(2)}) collective-permute-start(bf16[2,3,4096]{2,0,1:T(2,128)(2,1)S(1)} %slice_bitcast_fusion.3), channel_id=1, source_target_pairs={{0,1},{1,2},{2,3},{4,5},{5,6},{6,7},{8,9},{9,10},{10,11},{12,13},{... | collective-permute-start | bytes 147464 | tf_op jit(solution)/shard_map/ppermute | solution.py:162
  36.9 2.7 %copy-start = (f32[128,3,4096]{0,2,1:T(8,128)}, f32[128,3,4096]{0,2,1:T(8,128)S(1)}, u32[]{:S(2)}) copy-start(f32[128,3,4096]{0,2,1:T(8,128)S(1)} %fusion) | copy-start | bytes 18874372
  62.8 3.0 %copy-start.3 = (bf16[512,512]{1,0:T(8,128)(2,1)S(1)}, bf16[512,512]{1,0:T(8,128)(2,1)}, u32[]{:S(2)}) copy-start(bf16[512,512]{1,0:T(8,128)(2,1)} %constant.10) | copy-start | bytes 1572868
  62.8 3.0 %copy-start.1 = (f32[1024,1024]{1,0:T(8,128)S(1)}, f32[1024,1024]{1,0:T(8,128)}, u32[]{:S(2)}) copy-start(f32[1024,1024]{1,0:T(8,128)} %fusion.8) | copy-start | bytes 12582916
  65.8 1.0 %copy-start.2 = (bf16[512,512]{1,0:T(8,128)(2,1)S(1)}, bf16[512,512]{1,0:T(8,128)(2,1)}, u32[]{:S(2)}) copy-start(bf16[512,512]{1,0:T(8,128)(2,1)} %constant.11) | copy-start | bytes 1572868
  65.8 1.0 %copy-start.4 = (f32[1024]{0:T(1024)S(1)}, f32[1024]{0:T(1024)}, u32[]{:S(2)}) copy-start(f32[1024]{0:T(1024)} %param.9) | copy-start | bytes 12292
Sparse Core Ops, SparseCore 0:
  10.0 42.7 all-gather.1
where the time goes:
time: 98.7 us; the launch traced here: 98.3 us
  blocking collectives  40.9 us (41%)
  other arithmetic  17.3 us (18%)
  local copies, waits for them, and re-layouts  15.1 us (15%)
  between operations  13.5 us (14%)
  matrix products  9.08 us (9%)
  starting transfers between devices  2.36 us (2%)
    all_to_all x1, blocking collectives, on_device(): lax.all_to_all(gated, 'ctx', split_axis=1, concat_axis=0, tiled=True)  16.9 us
    all_to_all x1, blocking collectives, on_device(): lax.all_to_all(response_slab, 'ctx', split_axis=0, concat_axis=1, tiled=T...  16.9 us
    add x1, other arithmetic, causal_short(): summed = summed + taps[tap_index] * widened[offset:offset + row_count]  9.39 us
    all_gather x1, blocking collectives, on_device(): all_taps = lax.all_gather(short_taps, 'ctx', axis=2, tiled=True)  7.11 us
    unnamed x11, local copies, waits for them, and re-layouts  6.44 us
    dot_general x1, matrix products, long_convolve(): sig = jnp.dot(forward, gated_slab, preferred_element_type=jnp.float32)  4.5 us
    convert_element_type x1, other arithmetic, causal_short(): widened = extended.astype(jnp.float32)  4.08 us
    dot_general x1, matrix products, long_convolve(): ker = jnp.dot(forward, filter_slab, preferred_element_type=jnp.float32)  2.94 us
  transfers between devices with their start and end apart: 2, of which 0 were waited for; matrix products, arithmetic and copies ran while one was open for 27% of the time, Pallas kernels for 0%

commit v1 on v0

--- a/solution.py
+++ b/solution.py
@@ -7,6 +7,29 @@
 
 RADIX = 64
 HIGH = lax.Precision.HIGHEST
+
+
+def in_order(blocks, dim):
+    lengths = list(blocks.shape[1:])
+    lengths[dim] *= blocks.shape[0]
+    return jnp.moveaxis(blocks, 0, dim).reshape(lengths)
+
+
+def collected_by_bits(x, axis):
+    length, position = (lax.axis_size(axis), lax.axis_index(axis))
+    blocks, bit = (x[None], 1)
+    while bit < length:
+        received = lax.ppermute(blocks, axis, [(i, i ^ bit) for i in range(length)])
+        low = position & bit == 0
+        blocks = jnp.concatenate(
+            [jnp.where(low, blocks, received), jnp.where(low, received, blocks)]
+        )
+        bit *= 2
+    return blocks
+
+
+def collect(array, axis, dim):
+    return in_order(collected_by_bits(array, axis), dim)
 
 
 def causal_short(extended, taps, kernel_size):
@@ -158,7 +181,7 @@
     ctx_size = lax.axis_size("ctx")
     rows = projected[0]
     filter_slab = lax.all_gather(long_filter, "dp", axis=0, tiled=True)
-    all_taps = lax.all_gather(short_taps, "ctx", axis=2, tiled=True)
+    all_taps = collect(short_taps, "ctx", 2)
     halo = lax.ppermute(
         rows[-(kernel_size - 1) :], "ctx", [(i, i + 1) for i in range(ctx_size - 1)]
     )

time: 98.7 us -> 94.9 us (0.961)
  blocking collectives: 40.9 us -> 33.8 us
  starting transfers between devices: 2.36 us -> 5.42 us
    all_gather x1 -> x0, blocking collectives: 7.11 us -> none  [on_device(): all_taps = lax.all_gather(short_taps, 'ctx', axis=2, tiled=True)]
    ppermute x0 -> x2, starting transfers between devices: none -> 3.46 us  [collected_by_bits(): received = lax.ppermute(blocks, axis, [(i, i ^ bit) for i in range(length)])]
    unnamed x11 -> x13, local copies, waits for them, and re-layouts: 6.44 us -> 6.41 us
  transfers between devices with their start and end apart: 2 -> 4, of which waited for: 0 -> 0; matrix products, arithmetic and copies ran while one was open for 27% -> 29% of each run, Pallas kernels for 0% -> 0%
where the time goes in v1:
time: 94.9 us; the launch traced here: 94.5 us
  blocking collectives  33.8 us (36%)
  other arithmetic  17.5 us (18%)
  local copies, waits for them, and re-layouts  15.1 us (16%)
  between operations  13.6 us (14%)
  matrix products  9.1 us (10%)
  starting transfers between devices  5.42 us (6%)
    all_to_all x1, blocking collectives, on_device(): lax.all_to_all(gated, 'ctx', split_axis=1, concat_axis=0, tiled=True)  16.9 us
    all_to_all x1, blocking collectives, on_device(): lax.all_to_all(response_slab, 'ctx', split_axis=0, concat_axis=1, tiled=T...  16.9 us
    add x1, other arithmetic, causal_short(): summed = summed + taps[tap_index] * widened[offset:offset + row_count]  9.39 us
    unnamed x13, local copies, waits for them, and re-layouts  6.41 us
    dot_general x1, matrix products, long_convolve(): sig = jnp.dot(forward, gated_slab, preferred_element_type=jnp.float32)  4.52 us
    convert_element_type x1, other arithmetic, causal_short(): widened = extended.astype(jnp.float32)  4.15 us
    ppermute x2, starting transfers between devices, collected_by_bits(): received = lax.ppermute(blocks, axis, [(i, i ^ bit) for i in range(length)])  3.46 us
    dot_general x1, matrix products, long_convolve(): ker = jnp.dot(forward, filter_slab, preferred_element_type=jnp.float32)  2.94 us
  transfers between devices with their start and end apart: 4, of which 0 were waited for; matrix products, arithmetic and copies ran while one was open for 29% of the time, Pallas kernels for 0%

profile of v1, /device:TPU:0, one launch (start us, length us, event | category | flops | bytes accessed | tf_op | source)
XLA Modules:
  0.0 94.5 jit_solution(17045763314938171059)
XLA Ops:
  6.5 0.0 all-gather.2.cloned.1.call-start
  6.5 0.5 collective-permute-start
  7.0 1.0 %slice_bitcast_fusion = bf16[2,3,4096]{2,0,1:T(2,128)(2,1)S(1)} fusion(bf16[1,128,3,4096]{3,1,2,0:T(8,128)(2,1)} %param.6), kind=kLoop, calls=%fused_computation.21 | loop fusion | bytes 98304 | tf_op jit(solution)/shard_map/slice | solution.py:186
  8.0 2.0 %collective-permute-start.2 = (bf16[2,3,4096]{2,0,1:T(2,128)(2,1)S(1)}, bf16[2,3,4096]{2,0,1:T(2,128)(2,1)S(1)}, u32[]{:S(2)}, u32[]{:S(2)}) collective-permute-start(bf16[2,3,4096]{2,0,1:T(2,128)(2,1)S(1)} %slice_bitcast_fusion), channel_id=1, source_target_pairs={{0,1},{1,2},{2,3},{4,5},{5,6},{6,7},{8,9},{9,10},{10,11},{12,13},{... | collective-permute-start | bytes 147464 | tf_op jit(solution)/shard_map/ppermute | solution.py:185
  9.9 0.0 all-gather.2.cloned.1.call-update
  10.0 0.0 copy-start.4
  10.0 3.5 %copy.19 = bf16[1,128,3,4096]{1,3,2,0:T(8,128)(2,1)S(1)} copy(bf16[1,128,3,4096]{3,1,2,0:T(8,128)(2,1)} %param.6) | data formatting | bytes 6291456 | tf_op args[0]
  13.5 0.0 collective-permute-done
  13.5 0.0 copy-done.4
  13.6 3.0 %collective-permute-start.1 = (f32[2,3,3,1024]{3,2,1,0:T(4,128)S(1)}, f32[2,3,3,1024]{3,2,1,0:T(4,128)S(1)}, u32[]{:S(2)}, u32[]{:S(2)}) collective-permute-start(f32[2,3,3,1024]{3,2,1,0:T(4,128)S(1)} %pad_maximum_fusion), channel_id=1, source_target_pairs={{0,2},{1,3},{2,0},{3,1},{4,6},{5,7},{6,4},{7,5},{8,10},{9,11},{10,... | collective-permute-start | bytes 221192 | tf_op jit(solution)/shard_map/ppermute | solution.py:22
  16.6 0.0 collective-permute-done.2
  16.6 2.8 %copy.20 = bf16[2,3,4096]{0,2,1:T(8,128)(2,1)} copy(bf16[2,3,4096]{2,0,1:T(2,128)(2,1)S(1)} %collective-permute-done.2) | data formatting | bytes 98304 | tf_op jit(solution)/shard_map/ppermute | solution.py:185
  19.4 4.1 %maximum_convert_fusion = f32[130,3,4096]{0,2,1:T(8,128)S(1)} fusion(bf16[128,3,4096]{0,2,1:T(8,128)(2,1)S(1)} %bitcast.38, bf16[2,3,4096]{0,2,1:T(8,128)(2,1)} %copy.20), kind=kLoop, calls=%fused_computation.5 | loop fusion | flops 6389760 | bytes 9584640 | tf_op jit(solution)/shard_map/convert_element_type | solution.py:37
  23.5 0.0 collective-permute-done.1
  23.7 9.4 %fusion = f32[128,3,4096]{0,2,1:T(8,128)S(1)} fusion(f32[130,3,4096]{0,2,1:T(8,128)S(1)} %maximum_convert_fusion, f32[3,4096]{1,0:T(4,128)S(1)} %bitcast.42, f32[3,4096]{1,0:T(4,128)S(1)} %bitcast.43, f32[3,4096]{1,0:T(4,128)S(1)} %bitcast.41), kind=kLoop, calls=%fused_computation.1 | loop fusion | flops 7864320 | bytes 25313280 | tf_op jit(solution)/shard_map/add | solution.py:41
  33.1 0.0 copy-start
  33.1 2.6 %copy-done = f32[128,3,4096]{0,2,1:T(8,128)} copy-done((f32[128,3,4096]{0,2,1:T(8,128)}, f32[128,3,4096]{0,2,1:T(8,128)S(1)}, u32[]{:S(2)}) %copy-start) | copy-done | bytes 6291480
  35.7 0.2 fusion.2
  35.9 0.5 copy.21
  36.5 16.9 %all_to_all.29 = bf16[128,4,1024]{2,0,1:T(8,128)(2,1)S(1)} all-to-all(bf16[128,4,1024]{2,0,1:T(8,128)(2,1)S(1)} %copy.21), channel_id=1, replica_groups=mesh['dp'=8,'ctx'=4] {'ctx'}, dimensions={1} | all-to-all | bytes 2097152 | tf_op jit(solution)/shard_map/all_to_all | solution.py:189
  53.4 0.8 copy.22
  54.2 0.3 reshape.53
  54.5 4.5 %fusion.9 = f32[1024,1024]{1,0:T(8,128)} fusion(bf16[1024,512]{1,0:T(8,128)(2,1)} %constant.19, bf16[512,1024]{1,0:T(8,128)(2,1)S(1)} %reshape.53), kind=kOutput, calls=%fused_computation.27 | convolution fusion | flops 1073741824 | bytes 6291456 | tf_op jit(solution)/shard_map/dot_general | solution.py:154
  59.0 0.0 copy-start.3
  59.0 0.0 all-gather.2.cloned.1.call-done
  59.0 0.0 copy-start.1
  59.0 2.9 %fusion.10 = f32[1024,1024]{1,0:T(8,128)S(1)} fusion(bf16[1024,512]{1,0:T(8,128)(2,1)} %constant.14.clone, bf16[512,1024]{1,0:T(8,128)(2,1)} %all-gather.2.cloned.1.call-done), kind=kOutput, calls=%fused_computation.28 | convolution fusion | flops 1073741824 | bytes 6291456 | tf_op jit(solution)/shard_map/dot_general | solution.py:155
  61.9 0.0 copy-done.3
  61.9 0.0 copy-done.1
  62.0 0.0 copy-start.2
  62.0 0.0 copy-start.5
  62.0 0.8 fusion.6
  62.8 0.2 copy-done.2
  63.0 0.0 copy-done.5
  63.0 0.9 fusion.4
  63.9 16.9 %all_to_all.30 = bf16[4,128,1024]{2,1,0:T(8,128)(2,1)S(1)} all-to-all(bf16[4,128,1024]{2,1,0:T(8,128)(2,1)S(1)} %bitcast.40), channel_id=1, replica_groups=mesh['dp'=8,'ctx'=4] {'ctx'}, dimensions={0} | all-to-all | bytes 2097152 | tf_op jit(solution)/shard_map/all_to_all | solution.py:191
  80.8 1.6 %convert_bitcast_fusion = f32[128,4,1024]{2,0,1:T(8,128)} fusion(bf16[4,128,1024]{2,1,0:T(8,128)(2,1)S(1)} %all_to_all.30), kind=kLoop, calls=%fused_computation.14 | loop fusion | flops 524288 | bytes 3145728 | tf_op jit(solution)/shard_map/convert_element_type | solution.py:176
  82.4 1.9 %copy.23 = f32[128,4,1024]{0,2,1:T(8,128)S(1)} copy(f32[128,4,1024]{2,0,1:T(8,128)} %convert_bitcast_fusion) | data formatting | bytes 4194304 | tf_op jit(solution)/shard_map/convert_element_type | solution.py:176
  84.3 2.0 %fusion.5 = bf16[1,128,4096]{1,2,0:T(8,128)(2,1)S(1)} fusion(f32[128,4,1024]{0,2,1:T(8,128)S(1)} %copy.23, f32[128,3,4096]{0,2,1:T(8,128)} %copy-done), kind=kLoop, calls=%fused_computation.13 | loop fusion | flops 1572864 | bytes 4194304 | tf_op jit(solution)/shard_map/convert_element_type | solution.py:176
  86.3 1.3 %copy.24 = bf16[1,128,4096]{2,1,0:T(8,128)(2,1)} copy(bf16[1,128,4096]{1,2,0:T(8,128)(2,1)S(1)} %fusion.5) | data formatting | bytes 2097152 | tf_op jit(solution)/shard_map/convert_element_type | solution.py:176
  (5 shorter events, 0.2 us)
Async XLA Ops:
  6.5 52.5 %all-gather.2.cloned.1.call-start = ((), (), s32[]{:S(2)}) async-start(), calls=%async_computation.2 | async-start | bytes 1179648 | tf_op jit(solution)/shard_map/all_gather | solution.py:183
  6.5 7.0 %collective-permute-start = (f32[1,3,3,1024]{3,2,1,0:T(4,128)}, f32[1,3,3,1024]{3,2,1,0:T(4,128)S(1)}, u32[]{:S(2)}, u32[]{:S(2)}) collective-permute-start(f32[1,3,3,1024]{3,2,1,0:T(4,128)} %bitcast.44), channel_id=1, source_target_pairs={{0,1},{1,0},{2,3},{3,2},{4,5},{5,4},{6,7},{7,6},{8,9},{9,8},{10,11... | collective-permute-start | bytes 110600 | tf_op jit(solution)/shard_map/ppermute | solution.py:22
  8.0 8.6 %collective-permute-start.2 = (bf16[2,3,4096]{2,0,1:T(2,128)(2,1)S(1)}, bf16[2,3,4096]{2,0,1:T(2,128)(2,1)S(1)}, u32[]{:S(2)}, u32[]{:S(2)}) collective-permute-start(bf16[2,3,4096]{2,0,1:T(2,128)(2,1)S(1)} %slice_bitcast_fusion), channel_id=1, source_target_pairs={{0,1},{1,2},{2,3},{4,5},{5,6},{6,7},{8,9},{9,10},{10,11},{12,13},{... | collective-permute-start | bytes 147464 | tf_op jit(solution)/shard_map/ppermute | solution.py:185
  10.0 3.5 %copy-start.4 = (f32[3,3,1024]{2,1,0:T(4,128)S(1)}, f32[3,3,1024]{2,1,0:T(4,128)}, u32[]{:S(2)}) copy-start(f32[3,3,1024]{2,1,0:T(4,128)} %param.7) | copy-start | bytes 110596
  13.6 10.0 %collective-permute-start.1 = (f32[2,3,3,1024]{3,2,1,0:T(4,128)S(1)}, f32[2,3,3,1024]{3,2,1,0:T(4,128)S(1)}, u32[]{:S(2)}, u32[]{:S(2)}) collective-permute-start(f32[2,3,3,1024]{3,2,1,0:T(4,128)S(1)} %pad_maximum_fusion), channel_id=1, source_target_pairs={{0,2},{1,3},{2,0},{3,1},{4,6},{5,7},{6,4},{7,5},{8,10},{9,11},{10,... | collective-permute-start | bytes 221192 | tf_op jit(solution)/shard_map/ppermute | solution.py:22
  33.1 2.6 %copy-start = (f32[128,3,4096]{0,2,1:T(8,128)}, f32[128,3,4096]{0,2,1:T(8,128)S(1)}, u32[]{:S(2)}) copy-start(f32[128,3,4096]{0,2,1:T(8,128)S(1)} %fusion) | copy-start | bytes 18874372
  59.0 3.0 %copy-start.3 = (bf16[512,512]{1,0:T(8,128)(2,1)S(1)}, bf16[512,512]{1,0:T(8,128)(2,1)}, u32[]{:S(2)}) copy-start(bf16[512,512]{1,0:T(8,128)(2,1)} %constant.20) | copy-start | bytes 1572868
  59.0 3.0 %copy-start.1 = (f32[1024,1024]{1,0:T(8,128)S(1)}, f32[1024,1024]{1,0:T(8,128)}, u32[]{:S(2)}) copy-start(f32[1024,1024]{1,0:T(8,128)} %fusion.9) | copy-start | bytes 12582916
  62.0 1.0 %copy-start.2 = (bf16[512,512]{1,0:T(8,128)(2,1)S(1)}, bf16[512,512]{1,0:T(8,128)(2,1)}, u32[]{:S(2)}) copy-start(bf16[512,512]{1,0:T(8,128)(2,1)} %constant.21) | copy-start | bytes 1572868
  62.0 1.0 %copy-start.5 = (f32[1024]{0:T(1024)S(1)}, f32[1024]{0:T(1024)}, u32[]{:S(2)}) copy-start(f32[1024]{0:T(1024)} %param.9) | copy-start | bytes 12292
Sparse Core Ops, SparseCore 0:
  10.1 42.8 all-gather.1
